TPU v7x, 512 devices: a whole 4x4x16 slice. The times are simulated.
512 devices in a mesh: grp: 16 (over y_lo, x, core), ep: 32 (over z, y_hi).
Axes of the slice: x: 4, y: 4 (y_hi: 2, y_lo: 2; y = y_hi * 2 + y_lo), z: 16, core: 2. Of those that a mesh axis runs over, the one named last changes fastest.
Arguments:
- tokens: bfloat16 [16, 512, 5120], P('grp', 'ep'), may hold values from -6 to 6
- cotangent: bfloat16 [16, 512, 5120], P('grp', 'ep'), may hold values from -1.5 to 1.5
- counts: int32 [16, 32, 4], P('grp', 'ep'), may hold values from 0 to 4, as said below
- destination: int32 [16, 32, 16], P('grp', 'ep'), may hold values from 0 to 15, each once within a row
- placement: int32 [32], replicated, may hold values from 0 to 31, each once
- gate_up_weight: bfloat16 [32, 2, 5120, 128], P('ep', None, 'grp'), may hold values from -0.078125 to 0.078125
- down_weight: bfloat16 [32, 5120, 128], P('ep', 'grp'), may hold values from -0.1875 to 0.1875
Outputs:
- layer_out: bfloat16 [16, 512, 5120], P('grp', 'ep')
- input_grad: bfloat16 [16, 512, 5120], P('grp', 'ep')
- gate_up_grad: float32 [32, 2, 5120, 128], P('ep', None, 'grp')
- down_grad: float32 [32, 5120, 128], P('ep', 'grp')
Inputs may be any that keep to these rules, and one draw needn't show every extreme that they name: counts[g, j, e] is the number of kept slots of expert e on device (g, j) after reassignment; some device has all 4 slots of an expert kept in every draw. `destination`: the 16 blocks of one device go to 16 different groups. `placement`: each expert slice is served by exactly one owner.
All inputs are finite; a program needn't handle non-finite values.
Results may differ from a plain program's by a relative error of at most 0.017.
Values may be sent and summed in bfloat16 or wider, within the bound.
No kernel may reach another device: no remote copies, remote signals or barrier semaphores. Data moves between devices by JAX's collectives and lax.ppermute only.
A program may use at most 64 MiB of HBM per device.

v0:
```python
import jax
import jax.numpy as jnp
from jax import lax
from jax.sharding import PartitionSpec as P


def swiglu_backward(gate_up, hidden_grad):
    gate_part = gate_up[0]
    up_part = gate_up[1]
    sigmoid_gate = jax.nn.sigmoid(gate_part)
    activated = gate_part * sigmoid_gate
    hidden = (activated * up_part).astype(jnp.bfloat16)
    gate_grad = hidden_grad * up_part * sigmoid_gate * (1.0 + gate_part * (1.0 - sigmoid_gate))
    up_grad = hidden_grad * activated
    return (hidden, jnp.stack([gate_grad, up_grad]).astype(jnp.bfloat16))


def body(tokens, cotangent, counts, destination, placement, gate_up_weight, down_weight):
    groups = lax.axis_size("grp")
    owners = lax.axis_size("ep")
    tok_dev = tokens.shape[1]
    model_width = tokens.shape[2]
    experts = counts.shape[2]
    capacity = tok_dev // experts
    block_rows = tok_dev // groups
    split_count = owners // experts
    row_count = owners * capacity
    order = jnp.argsort(destination[0, 0])
    send_tokens = jnp.take(tokens[0].reshape(groups, block_rows, model_width), order, axis=0)
    send_cotangent = jnp.take(cotangent[0].reshape(groups, block_rows, model_width), order, axis=0)
    here_tokens, here_cotangent = (
        lax.all_to_all(send_tokens, "grp", split_axis=0, concat_axis=0, tiled=True),
        lax.all_to_all(send_cotangent, "grp", split_axis=0, concat_axis=0, tiled=True),
    )
    slot_ids = lax.broadcasted_iota(jnp.int32, (experts, capacity), 1)
    keep = (slot_ids < counts[0, 0][:, None])[:, :, None]
    nothing = jnp.zeros((), jnp.bfloat16)
    kept_tokens = jnp.where(keep, here_tokens.reshape(experts, capacity, model_width), nothing)
    kept_cotangent = jnp.where(
        keep, here_cotangent.reshape(experts, capacity, model_width), nothing
    )
    expert_of = placement // split_count
    routed_tokens, routed_cotangent = (
        lax.all_to_all(
            jnp.take(kept_tokens, expert_of, axis=0), "ep", split_axis=0, concat_axis=0, tiled=True
        ),
        lax.all_to_all(
            jnp.take(kept_cotangent, expert_of, axis=0),
            "ep",
            split_axis=0,
            concat_axis=0,
            tiled=True,
        ),
    )
    routed_tokens = routed_tokens.reshape(row_count, model_width)
    routed_cotangent = routed_cotangent.reshape(row_count, model_width)
    stacked_down = down_weight[:, None]
    full_gate_up, full_down = (
        lax.all_gather(gate_up_weight, "grp", axis=2, tiled=True),
        lax.all_gather(stacked_down, "grp", axis=2, tiled=True),
    )
    full_gate_up = full_gate_up[0]
    full_down = full_down[0, 0]
    gate_up = jnp.einsum(
        "rd,kds->krs", routed_tokens, full_gate_up, preferred_element_type=jnp.float32
    )
    hidden_grad = jnp.dot(routed_cotangent, full_down, preferred_element_type=jnp.float32)
    hidden, grad_rows = swiglu_backward(gate_up, hidden_grad)
    forward_part = (
        jnp.einsum("rs,ds->rd", hidden, full_down, preferred_element_type=jnp.float32)
        .astype(jnp.bfloat16)
        .reshape(owners, capacity, model_width)
    )
    backward_part = (
        jnp.einsum("krs,kds->rd", grad_rows, full_gate_up, preferred_element_type=jnp.float32)
        .astype(jnp.bfloat16)
        .reshape(owners, capacity, model_width)
    )
    owner_table = (
        expert_of[:, None] == lax.broadcasted_iota(jnp.int32, (owners, experts), 1)
    ).astype(jnp.bfloat16)

    def combine(returned):
        summed = jnp.einsum(
            "jcd,je->ecd", returned, owner_table, preferred_element_type=jnp.float32
        )
        return summed.astype(jnp.bfloat16).reshape(1, tok_dev, model_width)

    layer_out = combine(lax.all_to_all(forward_part, "ep", split_axis=0, concat_axis=0, tiled=True))
    input_grad = combine(
        lax.all_to_all(backward_part, "ep", split_axis=0, concat_axis=0, tiled=True)
    )
    gate_up_term = jnp.einsum(
        "rd,krs->kds", routed_tokens, grad_rows, preferred_element_type=jnp.float32
    )
    down_term = jnp.einsum(
        "rd,rs->ds", routed_cotangent, hidden, preferred_element_type=jnp.float32
    )
    gate_up_grad, down_grad = (
        lax.psum_scatter(
            gate_up_term[None].astype(jnp.bfloat16), "grp", scatter_dimension=2, tiled=True
        ).astype(jnp.float32),
        lax.psum_scatter(
            down_term[None, None].astype(jnp.bfloat16), "grp", scatter_dimension=2, tiled=True
        ).astype(jnp.float32),
    )
    return (layer_out, input_grad, gate_up_grad, down_grad[:, 0])


def solution(mesh):
    return jax.shard_map(
        body,
        mesh=mesh,
        in_specs=(
            P("grp", "ep", None),
            P("grp", "ep", None),
            P("grp", "ep", None),
            P("grp", "ep", None),
            P(),
            P("ep", None, "grp", None),
            P("ep", "grp", None),
        ),
        out_specs=(
            P("grp", "ep", None),
            P("grp", "ep", None),
            P("ep", None, "grp", None),
            P("ep", "grp", None),
        ),
        check_vma=False,
    )
```

profile of v0, /device:TPU:32, one launch (start us, length us, event | category | flops | bytes accessed | tf_op | source)
XLA Modules:
  0.0 448.5 jit_solution(12998677638847090264)
XLA Ops:
  12.6 5.4 %all-to-all-start = ((bf16[16,2,2560]{2,1,0:T(2,128)(2,1)}), bf16[16,2,2560]{2,1,0:T(2,128)(2,1)S(1)}, u32[]{:S(2)}, u32[]{:S(2)}) async-start(bf16[16,2,2560]{2,1,0:T(2,128)(2,1)} %reshape.164), calls=%async_computation | async-start | bytes 327680 | tf_op jit(solution)/shard_map/all_to_all | solution.py:32
  19.6 5.2 %all-to-all-done = bf16[16,2,2560]{2,1,0:T(2,128)(2,1)S(1)} async-done(((bf16[16,2,2560]{2,1,0:T(2,128)(2,1)}), bf16[16,2,2560]{2,1,0:T(2,128)(2,1)S(1)}, u32[]{:S(2)}, u32[]{:S(2)}) %all-to-all-start) | async-done | bytes 163872 | tf_op jit(solution)/shard_map/all_to_all | solution.py:32
  24.8 3.5 all-to-all-start.3
  29.5 5.5 %all-to-all-done.3 = bf16[16,2,2560]{2,1,0:T(2,128)(2,1)S(1)} async-done(((bf16[16,2,2560]{2,1,0:T(2,128)(2,1)}), bf16[16,2,2560]{2,1,0:T(2,128)(2,1)S(1)}, u32[]{:S(2)}, u32[]{:S(2)}) %all-to-all-start.3) | async-done | bytes 163872 | tf_op jit(solution)/shard_map/all_to_all | solution.py:33
  39.8 2.7 broadcast_select_fusion
  42.5 17.7 %all-to-all-start.1 = ((bf16[32,4,5120]{2,1,0:T(4,128)(2,1)}), bf16[32,4,5120]{2,1,0:T(4,128)(2,1)S(1)}, u32[]{:S(2)}, u32[]{:S(2)}) async-start(bf16[32,4,5120]{2,1,0:T(4,128)(2,1)} %get-tuple-element.29), calls=%async_computation.1 | async-start | bytes 2621440 | tf_op jit(solution)/shard_map/all_to_all | solution.py:44
  60.9 64.1 %all-to-all-done.1 = bf16[32,4,5120]{2,1,0:T(4,128)(2,1)S(1)} async-done(((bf16[32,4,5120]{2,1,0:T(4,128)(2,1)}), bf16[32,4,5120]{2,1,0:T(4,128)(2,1)S(1)}, u32[]{:S(2)}, u32[]{:S(2)}) %all-to-all-start.1) | async-done | bytes 1310752 | tf_op jit(solution)/shard_map/all_to_all | solution.py:44
  126.1 6.9 %all-to-all-start.4 = ((bf16[32,4,5120]{2,1,0:T(4,128)(2,1)}), bf16[32,4,5120]{2,1,0:T(4,128)(2,1)S(1)}, u32[]{:S(2)}, u32[]{:S(2)}) async-start(bf16[32,4,5120]{2,1,0:T(4,128)(2,1)} %get-tuple-element.28), calls=%async_computation.4 | async-start | bytes 2621440 | tf_op jit(solution)/shard_map/all_to_all | solution.py:47
  133.8 2.5 reshape.157
  136.3 2.3 fusion.11
  138.6 37.2 %all-gather.6.cloned.1.call-done = bf16[1,5120,128]{2,1,0:T(8,128)(2,1)} async-done(((bf16[1,320,128]{2,1,0:T(8,128)(2,1)}), bf16[1,5120,128]{2,1,0:T(8,128)(2,1)}) %all-gather.6.cloned.1.call-update) | async-done | bytes 1310736 | tf_op jit(solution)/shard_map/all_gather | solution.py:60
  175.8 2.9 convolution_convert_fusion.2
  178.7 3.4 reshape.96
  182.1 15.2 %all-to-all-done.4 = bf16[32,4,5120]{2,1,0:T(4,128)(2,1)S(1)} async-done(((bf16[32,4,5120]{2,1,0:T(4,128)(2,1)}), bf16[32,4,5120]{2,1,0:T(4,128)(2,1)S(1)}, u32[]{:S(2)}, u32[]{:S(2)}) %all-to-all-start.4) | async-done | bytes 1310752 | tf_op jit(solution)/shard_map/all_to_all | solution.py:47
  198.3 7.1 %all-to-all-start.2 = ((bf16[32,4,5120]{2,1,0:T(4,128)(2,1)}), bf16[32,4,5120]{2,1,0:T(4,128)(2,1)}, u32[]{:S(2)}, u32[]{:S(2)}) async-start(bf16[32,4,5120]{2,1,0:T(4,128)(2,1)} %reshape.96), calls=%async_computation.2 | async-start | bytes 2621440 | tf_op jit(solution)/shard_map/all_to_all | solution.py:89
  205.6 2.5 reshape.99
  209.9 2.3 fusion
  212.3 7.4 %copy.37 = bf16[1,2,5120,128]{3,1,0,2:T(2,128)(2,1)} copy(bf16[1,2,5120,128]{2,3,1,0:T(8,128)(2,1)} %fusion) | data formatting | bytes 5242880 | tf_op jit(solution)/shard_map/convert_element_type | solution.py:101
  219.7 2.7 fusion.1
  223.8 46.0 %all-to-all-done.2 = bf16[32,4,5120]{2,1,0:T(4,128)(2,1)} async-done(((bf16[32,4,5120]{2,1,0:T(4,128)(2,1)}), bf16[32,4,5120]{2,1,0:T(4,128)(2,1)}, u32[]{:S(2)}, u32[]{:S(2)}) %all-to-all-start.2) | async-done | bytes 1310752 | tf_op jit(solution)/shard_map/all_to_all | solution.py:89
  269.8 7.0 %all-to-all-start.5 = ((bf16[32,4,5120]{2,1,0:T(4,128)(2,1)}), bf16[32,4,5120]{2,1,0:T(4,128)(2,1)S(1)}, u32[]{:S(2)}, u32[]{:S(2)}) async-start(bf16[32,4,5120]{2,1,0:T(4,128)(2,1)} %reshape.100), calls=%async_computation.5 | async-start | bytes 2621440 | tf_op jit(solution)/shard_map/all_to_all | solution.py:91
  280.4 81.9 %all-reduce.3.cloned.1.call-done = bf16[1,2,5120,128]{3,1,0,2:T(2,128)(2,1)} async-done(((bf16[1,2,5120,128]{3,1,0,2:T(2,128)(2,1)}), bf16[1,2,5120,128]{3,1,0,2:T(2,128)(2,1)}) %all-reduce.3.cloned.1.call-update) | async-done | bytes 2621456
  364.1 71.7 %reduce-scatter.2.cloned.1.call-done = bf16[1,1,320,128]{3,2,1,0:T(8,128)(2,1)} async-done(((bf16[1,1,5120,128]{3,2,1,0:T(8,128)(2,1)}), bf16[1,1,320,128]{3,2,1,0:T(8,128)(2,1)}) %reduce-scatter.2.cloned.1.call-update) | async-done | bytes 81936 | tf_op jit(solution)/shard_map/reduce_scatter | solution.py:103
  437.4 2.1 convolution_convert_fusion.4
  (61 shorter events, 28.5 us)
Async XLA Ops:
  7.2 2.0 copy-start
  7.2 2.7 copy-start.1
  9.8 8.2 %copy-start.4 = (s32[32]{0:T(128)S(1)}, s32[32]{0:T(128)}, u32[]{:S(2)}) copy-start(s32[32]{0:T(128)} %param.15) | copy-start | bytes 388
  10.5 9.1 %copy-start.5 = (s32[1,1,4]{2,1,0:T(1,128)S(1)}, s32[1,1,4]{2,1,0:T(1,128)}, u32[]{:S(2)}) copy-start(s32[1,1,4]{2,1,0:T(1,128)} %param.13) | copy-start | bytes 52
  12.6 12.2 %all-to-all-start = ((bf16[16,2,2560]{2,1,0:T(2,128)(2,1)}), bf16[16,2,2560]{2,1,0:T(2,128)(2,1)S(1)}, u32[]{:S(2)}, u32[]{:S(2)}) async-start(bf16[16,2,2560]{2,1,0:T(2,128)(2,1)} %reshape.164), calls=%async_computation | async-start | bytes 327680 | tf_op jit(solution)/shard_map/all_to_all | solution.py:32
  24.8 10.2 %all-to-all-start.3 = ((bf16[16,2,2560]{2,1,0:T(2,128)(2,1)}), bf16[16,2,2560]{2,1,0:T(2,128)(2,1)S(1)}, u32[]{:S(2)}, u32[]{:S(2)}) async-start(bf16[16,2,2560]{2,1,0:T(2,128)(2,1)} %reshape.166), calls=%async_computation.3 | async-start | bytes 327680 | tf_op jit(solution)/shard_map/all_to_all | solution.py:33
  42.5 82.5 %all-to-all-start.1 = ((bf16[32,4,5120]{2,1,0:T(4,128)(2,1)}), bf16[32,4,5120]{2,1,0:T(4,128)(2,1)S(1)}, u32[]{:S(2)}, u32[]{:S(2)}) async-start(bf16[32,4,5120]{2,1,0:T(4,128)(2,1)} %get-tuple-element.29), calls=%async_computation.1 | async-start | bytes 2621440 | tf_op jit(solution)/shard_map/all_to_all | solution.py:44
  60.2 76.1 %all-gather.4.cloned.1.call-start = ((), (), s32[]{:S(2)}) async-start(), calls=%async_computation.7 | async-start | bytes 2785280 | tf_op jit(solution)/shard_map/all_gather | solution.py:59
  125.0 1.1 copy-start.3
  126.1 71.2 %all-to-all-start.4 = ((bf16[32,4,5120]{2,1,0:T(4,128)(2,1)}), bf16[32,4,5120]{2,1,0:T(4,128)(2,1)S(1)}, u32[]{:S(2)}, u32[]{:S(2)}) async-start(bf16[32,4,5120]{2,1,0:T(4,128)(2,1)} %get-tuple-element.28), calls=%async_computation.4 | async-start | bytes 2621440 | tf_op jit(solution)/shard_map/all_to_all | solution.py:47
  133.0 42.7 %all-gather.6.cloned.1.call-start = ((), (), s32[]{:S(2)}) async-start(), calls=%async_computation.9 | async-start | bytes 1392640 | tf_op jit(solution)/shard_map/all_gather | solution.py:60
  197.3 1.0 copy-start.2
  198.3 71.5 %all-to-all-start.2 = ((bf16[32,4,5120]{2,1,0:T(4,128)(2,1)}), bf16[32,4,5120]{2,1,0:T(4,128)(2,1)}, u32[]{:S(2)}, u32[]{:S(2)}) async-start(bf16[32,4,5120]{2,1,0:T(4,128)(2,1)} %reshape.96), calls=%async_computation.2 | async-start | bytes 2621440 | tf_op jit(solution)/shard_map/all_to_all | solution.py:89
  205.4 156.9 %all-reduce.3.cloned.1.call-start = ((), (), s32[]{:S(2)}) async-start(), calls=%async_computation.10 | async-start | bytes 5242880
  269.8 170.5 %all-to-all-start.5 = ((bf16[32,4,5120]{2,1,0:T(4,128)(2,1)}), bf16[32,4,5120]{2,1,0:T(4,128)(2,1)S(1)}, u32[]{:S(2)}, u32[]{:S(2)}) async-start(bf16[32,4,5120]{2,1,0:T(4,128)(2,1)} %reshape.100), calls=%async_computation.5 | async-start | bytes 2621440 | tf_op jit(solution)/shard_map/all_to_all | solution.py:91
  276.8 159.0 %reduce-scatter.2.cloned.1.call-start = ((), (), s32[]{:S(2)}) async-start(), calls=%async_computation.8 | async-start | bytes 1392640 | tf_op jit(solution)/shard_map/reduce_scatter | solution.py:103
Sparse Core Ops, SparseCore 0:
  63.1 41.9 all-gather.3
  136.0 39.7 all-gather.5
  219.8 142.4 all-reduce.2
  365.0 70.7 reduce-scatter.1
where the time goes:
time: 450 us; the launch traced here: 448 us
  waiting for transfers between devices  328 us (73%)
  starting transfers between devices  48 us (11%)
  local copies, waits for them, and re-layouts  30 us (7%)
  matrix products  16.6 us (4%)
  between operations  14.7 us (3%)
  other arithmetic  11 us (2%)
    unnamed x5, waiting for transfers between devices  83.3 us
    reduce_scatter x1, waiting for transfers between devices, body(): lax.psum_scatter(down_term[None, None].astype(jnp.bfloat16), 'grp', scatt...  71.7 us
    all_to_all x1, waiting for transfers between devices, body(): lax.all_to_all(jnp.take(kept_tokens, expert_of, axis=0), 'ep', split_axis...  64.1 us
    all_to_all x1, waiting for transfers between devices, body(): lax.all_to_all(forward_part, 'ep', split_axis=0, concat_axis=0, tiled=True)  46 us
    all_gather x1, waiting for transfers between devices, body(): lax.all_gather(stacked_down, 'grp', axis=2, tiled=True)  37.2 us
    all_to_all x1, starting transfers between devices, body(): lax.all_to_all(jnp.take(kept_tokens, expert_of, axis=0), 'ep', split_axis...  17.7 us
    all_to_all x1, waiting for transfers between devices, body(): lax.all_to_all(jnp.take(kept_cotangent, expert_of, axis=0), 'ep', split_a...  15.2 us
  transfers between devices with their start and end apart: 10, of which 8 were waited for; matrix products, arithmetic and copies ran while one was open for 9% of the time, Pallas kernels for 0%

commit v1 on v0

--- a/solution.py
+++ b/solution.py
@@ -2,6 +2,13 @@
 import jax.numpy as jnp
 from jax import lax
 from jax.sharding import PartitionSpec as P
+
+
+def exchange_gather(x, axis, dim):
+    peers = lax.axis_size(axis)
+    pieces = jnp.stack([x for _ in range(peers)])
+    pieces = lax.all_to_all(pieces, axis, split_axis=0, concat_axis=0)
+    return jnp.concatenate(pieces, axis=dim)
 
 
 def swiglu_backward(gate_up, hidden_grad):
@@ -57,7 +64,7 @@
     stacked_down = down_weight[:, None]
     full_gate_up, full_down = (
         lax.all_gather(gate_up_weight, "grp", axis=2, tiled=True),
-        lax.all_gather(stacked_down, "grp", axis=2, tiled=True),
+        exchange_gather(stacked_down, "grp", 2),
     )
     full_gate_up = full_gate_up[0]
     full_down = full_down[0, 0]

time: 450 us -> 467 us (1.038)
  waiting for transfers between devices: 328 us -> 336 us
  local copies, waits for them, and re-layouts: 30 us -> 35.9 us
    all_to_all x1, waiting for transfers between devices: 15.2 us -> 54.5 us  [body(): lax.all_to_all(jnp.take(kept_cotangent, expert_of, axis=0), 'ep', split_a...]
    all_gather x1 -> x0, waiting for transfers between devices: 37.2 us -> none  [body(): lax.all_gather(stacked_down, 'grp', axis=2, tiled=True)]
    all_to_all x0 -> x1, waiting for transfers between devices: none -> 9.46 us  [exchange_gather(): pieces = lax.all_to_all(pieces, axis, split_axis=0, concat_axis=0)]
    unnamed x5 -> x4, waiting for transfers between devices: 83.3 us -> 83.6 us
  transfers between devices with their start and end apart: 10 -> 10, of which waited for: 8 -> 8; matrix products, arithmetic and copies ran while one was open for 9% -> 11% of each run, Pallas kernels for 0% -> 0%
where the time goes in v1:
time: 467 us; the launch traced here: 465 us
  waiting for transfers between devices  336 us (72%)
  starting transfers between devices  51.9 us (11%)
  local copies, waits for them, and re-layouts  35.9 us (8%)
  matrix products  14.7 us (3%)
  between operations  14.7 us (3%)
  other arithmetic  12.4 us (3%)
    unnamed x4, waiting for transfers between devices  83.6 us
    reduce_scatter x1, waiting for transfers between devices, body(): lax.psum_scatter(down_term[None, None].astype(jnp.bfloat16), 'grp', scatt...  71.8 us
    all_to_all x1, waiting for transfers between devices, body(): lax.all_to_all(jnp.take(kept_tokens, expert_of, axis=0), 'ep', split_axis...  63.8 us
    all_to_all x1, waiting for transfers between devices, body(): lax.all_to_all(jnp.take(kept_cotangent, expert_of, axis=0), 'ep', split_a...  54.5 us
    all_to_all x1, waiting for transfers between devices, body(): lax.all_to_all(forward_part, 'ep', split_axis=0, concat_axis=0, tiled=True)  42 us
    all_to_all x1, starting transfers between devices, body(): lax.all_to_all(jnp.take(kept_tokens, expert_of, axis=0), 'ep', split_axis...  17.7 us
    all_to_all x1, waiting for transfers between devices, exchange_gather(): pieces = lax.all_to_all(pieces, axis, split_axis=0, concat_axis=0)  9.46 us
  transfers between devices with their start and end apart: 10, of which 8 were waited for; matrix products, arithmetic and copies ran while one was open for 11% of the time, Pallas kernels for 0%

profile of v1, /device:TPU:32, one launch (start us, length us, event | category | flops | bytes accessed | tf_op | source)
XLA Modules:
  0.0 465.3 jit_solution(4263457984447374391)
XLA Ops:
  12.6 5.5 %all-to-all-start = ((bf16[16,2,2560]{2,1,0:T(2,128)(2,1)}), bf16[16,2,2560]{2,1,0:T(2,128)(2,1)S(1)}, u32[]{:S(2)}, u32[]{:S(2)}) async-start(bf16[16,2,2560]{2,1,0:T(2,128)(2,1)} %reshape.165), calls=%async_computation | async-start | bytes 327680 | tf_op jit(solution)/shard_map/all_to_all | solution.py:39
  19.8 5.2 %all-to-all-done = bf16[16,2,2560]{2,1,0:T(2,128)(2,1)S(1)} async-done(((bf16[16,2,2560]{2,1,0:T(2,128)(2,1)}), bf16[16,2,2560]{2,1,0:T(2,128)(2,1)S(1)}, u32[]{:S(2)}, u32[]{:S(2)}) %all-to-all-start) | async-done | bytes 163872 | tf_op jit(solution)/shard_map/all_to_all | solution.py:39
  24.9 3.5 all-to-all-start.4
  29.6 5.5 %all-to-all-done.4 = bf16[16,2,2560]{2,1,0:T(2,128)(2,1)S(1)} async-done(((bf16[16,2,2560]{2,1,0:T(2,128)(2,1)}), bf16[16,2,2560]{2,1,0:T(2,128)(2,1)S(1)}, u32[]{:S(2)}, u32[]{:S(2)}) %all-to-all-start.4) | async-done | bytes 163872 | tf_op jit(solution)/shard_map/all_to_all | solution.py:40
  36.5 3.7 all-to-all-start.2
  43.3 2.6 gather_fusion.1
  45.9 4.1 broadcast_select_fusion
  50.0 9.5 %all-to-all-done.2 = bf16[16,1,1,320,128]{4,3,2,1,0:T(8,128)(2,1)S(1)} async-done(((bf16[16,1,1,320,128]{4,3,2,1,0:T(8,128)(2,1)}), bf16[16,1,1,320,128]{4,3,2,1,0:T(8,128)(2,1)S(1)}, u32[]{:S(2)}, u32[]{:S(2)}) %all-to-all-start.2) | async-done | bytes 1310752 | tf_op jit(solution)/shard_map/all_to_all | solution.py:10
  59.4 17.7 %all-to-all-start.1 = ((bf16[32,4,5120]{2,1,0:T(4,128)(2,1)}), bf16[32,4,5120]{2,1,0:T(4,128)(2,1)S(1)}, u32[]{:S(2)}, u32[]{:S(2)}) async-start(bf16[32,4,5120]{2,1,0:T(4,128)(2,1)} %get-tuple-element.29), calls=%async_computation.1 | async-start | bytes 2621440 | tf_op jit(solution)/shard_map/all_to_all | solution.py:51
  77.9 63.8 %all-to-all-done.1 = bf16[32,4,5120]{2,1,0:T(4,128)(2,1)S(1)} async-done(((bf16[32,4,5120]{2,1,0:T(4,128)(2,1)}), bf16[32,4,5120]{2,1,0:T(4,128)(2,1)S(1)}, u32[]{:S(2)}, u32[]{:S(2)}) %all-to-all-start.1) | async-done | bytes 1310752 | tf_op jit(solution)/shard_map/all_to_all | solution.py:51
  142.8 7.0 %all-to-all-start.5 = ((bf16[32,4,5120]{2,1,0:T(4,128)(2,1)}), bf16[32,4,5120]{2,1,0:T(4,128)(2,1)}, u32[]{:S(2)}, u32[]{:S(2)}) async-start(bf16[32,4,5120]{2,1,0:T(4,128)(2,1)} %get-tuple-element.28), calls=%async_computation.5 | async-start | bytes 2621440 | tf_op jit(solution)/shard_map/all_to_all | solution.py:54
  149.8 2.5 reshape.158
  152.3 2.3 fusion.8
  156.2 3.4 reshape.99
  159.6 54.5 %all-to-all-done.5 = bf16[32,4,5120]{2,1,0:T(4,128)(2,1)} async-done(((bf16[32,4,5120]{2,1,0:T(4,128)(2,1)}), bf16[32,4,5120]{2,1,0:T(4,128)(2,1)}, u32[]{:S(2)}, u32[]{:S(2)}) %all-to-all-start.5) | async-done | bytes 1310752 | tf_op jit(solution)/shard_map/all_to_all | solution.py:54
  214.1 7.1 %all-to-all-start.3 = ((bf16[32,4,5120]{2,1,0:T(4,128)(2,1)}), bf16[32,4,5120]{2,1,0:T(4,128)(2,1)}, u32[]{:S(2)}, u32[]{:S(2)}) async-start(bf16[32,4,5120]{2,1,0:T(4,128)(2,1)} %reshape.99), calls=%async_computation.3 | async-start | bytes 2621440 | tf_op jit(solution)/shard_map/all_to_all | solution.py:96
  221.4 3.3 reshape.102
  226.5 2.4 fusion
  228.9 7.4 %copy.37 = bf16[1,2,5120,128]{3,1,0,2:T(2,128)(2,1)} copy(bf16[1,2,5120,128]{2,3,1,0:T(8,128)(2,1)} %fusion) | data formatting | bytes 5242880 | tf_op jit(solution)/shard_map/convert_element_type | solution.py:108
  240.1 3.4 reshape.103
  243.5 42.0 %all-to-all-done.3 = bf16[32,4,5120]{2,1,0:T(4,128)(2,1)} async-done(((bf16[32,4,5120]{2,1,0:T(4,128)(2,1)}), bf16[32,4,5120]{2,1,0:T(4,128)(2,1)}, u32[]{:S(2)}, u32[]{:S(2)}) %all-to-all-start.3) | async-done | bytes 1310752 | tf_op jit(solution)/shard_map/all_to_all | solution.py:96
  285.6 7.0 %all-to-all-start.6 = ((bf16[32,4,5120]{2,1,0:T(4,128)(2,1)}), bf16[32,4,5120]{2,1,0:T(4,128)(2,1)S(1)}, u32[]{:S(2)}, u32[]{:S(2)}) async-start(bf16[32,4,5120]{2,1,0:T(4,128)(2,1)} %reshape.103), calls=%async_computation.6 | async-start | bytes 2621440 | tf_op jit(solution)/shard_map/all_to_all | solution.py:98
  296.3 82.9 %all-reduce.3.cloned.1.call-done = bf16[1,2,5120,128]{3,1,0,2:T(2,128)(2,1)} async-done(((bf16[1,2,5120,128]{3,1,0,2:T(2,128)(2,1)}), bf16[1,2,5120,128]{3,1,0,2:T(2,128)(2,1)}) %all-reduce.3.cloned.1.call-update) | async-done | bytes 2621456
  380.9 71.8 %reduce-scatter.2.cloned.1.call-done = bf16[1,1,320,128]{3,2,1,0:T(8,128)(2,1)} async-done(((bf16[1,1,5120,128]{3,2,1,0:T(8,128)(2,1)}), bf16[1,1,320,128]{3,2,1,0:T(8,128)(2,1)}) %reduce-scatter.2.cloned.1.call-update) | async-done | bytes 81936 | tf_op jit(solution)/shard_map/reduce_scatter | solution.py:110
  (65 shorter events, 32.6 us)
Async XLA Ops:
  7.2 2.0 copy-start
  7.2 2.7 copy-start.2
  9.8 8.3 %copy-start.6 = (s32[32]{0:T(128)S(1)}, s32[32]{0:T(128)}, u32[]{:S(2)}) copy-start(s32[32]{0:T(128)} %param.15) | copy-start | bytes 388
  10.5 9.2 %copy-start.7 = (s32[1,1,4]{2,1,0:T(1,128)S(1)}, s32[1,1,4]{2,1,0:T(1,128)}, u32[]{:S(2)}) copy-start(s32[1,1,4]{2,1,0:T(1,128)} %param.13) | copy-start | bytes 52
  12.6 22.5 %copy-start.5 = (bf16[1,320,128]{2,1,0:T(8,128)(2,1)S(1)}, bf16[1,320,128]{2,1,0:T(8,128)(2,1)}, u32[]{:S(2)}) copy-start(bf16[1,320,128]{2,1,0:T(8,128)(2,1)} %param.17) | copy-start | bytes 245764
  12.6 12.3 %all-to-all-start = ((bf16[16,2,2560]{2,1,0:T(2,128)(2,1)}), bf16[16,2,2560]{2,1,0:T(2,128)(2,1)S(1)}, u32[]{:S(2)}, u32[]{:S(2)}) async-start(bf16[16,2,2560]{2,1,0:T(2,128)(2,1)} %reshape.165), calls=%async_computation | async-start | bytes 327680 | tf_op jit(solution)/shard_map/all_to_all | solution.py:39
  24.9 10.2 %all-to-all-start.4 = ((bf16[16,2,2560]{2,1,0:T(2,128)(2,1)}), bf16[16,2,2560]{2,1,0:T(2,128)(2,1)S(1)}, u32[]{:S(2)}, u32[]{:S(2)}) async-start(bf16[16,2,2560]{2,1,0:T(2,128)(2,1)} %reshape.167), calls=%async_computation.4 | async-start | bytes 327680 | tf_op jit(solution)/shard_map/all_to_all | solution.py:40
  36.5 22.9 %all-to-all-start.2 = ((bf16[16,1,1,320,128]{4,3,2,1,0:T(8,128)(2,1)}), bf16[16,1,1,320,128]{4,3,2,1,0:T(8,128)(2,1)S(1)}, u32[]{:S(2)}, u32[]{:S(2)}) async-start(bf16[16,1,1,320,128]{4,3,2,1,0:T(8,128)(2,1)} %stack.15), calls=%async_computation.2 | async-start | bytes 2621440 | tf_op jit(solution)/shard_map/all_to_all | solution.py:10
  59.4 82.2 %all-to-all-start.1 = ((bf16[32,4,5120]{2,1,0:T(4,128)(2,1)}), bf16[32,4,5120]{2,1,0:T(4,128)(2,1)S(1)}, u32[]{:S(2)}, u32[]{:S(2)}) async-start(bf16[32,4,5120]{2,1,0:T(4,128)(2,1)} %get-tuple-element.29), calls=%async_computation.1 | async-start | bytes 2621440 | tf_op jit(solution)/shard_map/all_to_all | solution.py:51
  77.1 75.2 %all-gather.2.cloned.1.call-start = ((), (), s32[]{:S(2)}) async-start(), calls=%async_computation.8 | async-start | bytes 2785280 | tf_op jit(solution)/shard_map/all_gather | solution.py:66
  141.7 1.1 copy-start.4
  142.8 71.4 %all-to-all-start.5 = ((bf16[32,4,5120]{2,1,0:T(4,128)(2,1)}), bf16[32,4,5120]{2,1,0:T(4,128)(2,1)}, u32[]{:S(2)}, u32[]{:S(2)}) async-start(bf16[32,4,5120]{2,1,0:T(4,128)(2,1)} %get-tuple-element.28), calls=%async_computation.5 | async-start | bytes 2621440 | tf_op jit(solution)/shard_map/all_to_all | solution.py:54
  214.1 71.5 %all-to-all-start.3 = ((bf16[32,4,5120]{2,1,0:T(4,128)(2,1)}), bf16[32,4,5120]{2,1,0:T(4,128)(2,1)}, u32[]{:S(2)}, u32[]{:S(2)}) async-start(bf16[32,4,5120]{2,1,0:T(4,128)(2,1)} %reshape.99), calls=%async_computation.3 | async-start | bytes 2621440 | tf_op jit(solution)/shard_map/all_to_all | solution.py:96
  221.2 157.9 %all-reduce.3.cloned.1.call-start = ((), (), s32[]{:S(2)}) async-start(), calls=%async_computation.10 | async-start | bytes 5242880
  236.3 1.7 copy-start.3
  243.5 49.1 %copy-start.1 = (bf16[128,5120]{1,0:T(8,128)(2,1)S(1)}, bf16[128,5120]{1,0:T(8,128)(2,1)}, u32[]{:S(2)}) copy-start(bf16[128,5120]{1,0:T(8,128)(2,1)} %reshape.102) | copy-start | bytes 3932164
  285.6 171.6 %all-to-all-start.6 = ((bf16[32,4,5120]{2,1,0:T(4,128)(2,1)}), bf16[32,4,5120]{2,1,0:T(4,128)(2,1)S(1)}, u32[]{:S(2)}, u32[]{:S(2)}) async-start(bf16[32,4,5120]{2,1,0:T(4,128)(2,1)} %reshape.103), calls=%async_computation.6 | async-start | bytes 2621440 | tf_op jit(solution)/shard_map/all_to_all | solution.py:98
  292.6 160.0 %reduce-scatter.2.cloned.1.call-start = ((), (), s32[]{:S(2)}) async-start(), calls=%async_computation.9 | async-start | bytes 1392640 | tf_op jit(solution)/shard_map/reduce_scatter | solution.py:110
Sparse Core Ops, SparseCore 0:
  80.1 41.4 all-gather.1
  236.5 142.5 all-reduce.2
  381.9 70.6 reduce-scatter.1
